TPU v7x, 32 devices: a whole 2x2x4 slice. The times are simulated.
32 devices in a mesh: section: 2 (over x), dp: 4 (over z), fsdp: 4 (over y, core).
Axes of the slice: x: 2, y: 2, z: 4, core: 2. Of those that a mesh axis runs over, the one named last changes fastest.
Arguments:
- inputs: float32 [32, 128, 1536], P(('dp', 'fsdp')), may hold values from -6 to 6
- cotangent: float32 [32, 128, 1536], P(('dp', 'fsdp')), may hold values from -6 to 6
- lengths: int32 [32], P(('dp', 'fsdp')), may hold values from 1 to 128, 2560 in all
- norm_gain: float32 [2, 1536], P('section'), may hold values from 0.5 to 1.5
- in_weight: bfloat16 [2, 1536, 6400], P('section', 'fsdp'), may hold values from -0.15625 to 0.15625
- dt_weight: bfloat16 [2, 1536, 48], P('section', 'fsdp'), may hold values from -0.15625 to 0.15625
- conv_weight: float32 [2, 4, 3328], P('section'), may hold values from -3 to 3
- conv_bias: float32 [2, 3328], P('section'), may hold values from -0.5 to 0.5
- dt_bias: float32 [2, 48], P('section'), may hold values from -4 to -1
- decay_log: float32 [2, 48], P('section'), may hold values from -4.6 to 0
- skip_gain: float32 [2, 48], P('section'), may hold values from 0.5 to 1.5
- gate_gain: float32 [2, 3072], P('section'), may hold values from 0.5 to 1.5
- out_weight: bfloat16 [2, 3072, 1536], P('section', 'fsdp'), may hold values from -0.109375 to 0.109375
Outputs:
- layer_outputs: float32 [2, 32, 128, 1536], P('section', ('dp', 'fsdp'))
- input_grads: float32 [2, 32, 128, 1536], P('section', ('dp', 'fsdp'))
- grad_norm_gain: float32 [2, 1536], P('section')
- grad_in_weight: float32 [2, 1536, 6400], P('section', 'fsdp')
- grad_dt_weight: float32 [2, 1536, 48], P('section', 'fsdp')
- grad_conv_weight: float32 [2, 4, 3328], P('section')
- grad_conv_bias: float32 [2, 3328], P('section')
- grad_dt_bias: float32 [2, 48], P('section')
- grad_decay_log: float32 [2, 48], P('section')
- grad_skip_gain: float32 [2, 48], P('section')
- grad_gate_gain: float32 [2, 3072], P('section')
- grad_out_weight: float32 [2, 3072, 1536], P('section', 'fsdp')
Inputs may be any that keep to these rules, and one draw needn't show every extreme that they name: `lengths`: positions from a sequence's length on are padding.
All inputs are finite; a program needn't handle non-finite values. No bound on the sum of `lengths` on one device may be relied on, other than what follows from the above.
Results may differ from a plain program's by a relative error of at most 0.011.
Values may be sent and summed in bfloat16 or wider, within the bound.
No kernel may reach another device: no remote copies, remote signals or barrier semaphores. Data moves between devices by JAX's collectives and lax.ppermute only.
A program may use at most 448 MiB of HBM per device.

v0:
```python
import jax
import jax.numpy as jnp
from jax import lax
from jax.sharding import PartitionSpec as P

INNER = 3072
HEADS = 48
HEAD_DIM = 64
STATE = 128
BLOCK = 64
CONV = 4
BUCKET = 128
MICRO = 2
epsilon = 1e-05
highest = lax.Precision.HIGHEST


def passed_along(block, axis, distance):
    devices = range(lax.axis_size(axis))
    route = [(i - distance, i) for i in devices if i - distance in devices]
    return lax.ppermute(block, axis, route)


def front_norm(residual, norm_gain):
    inverse = lax.rsqrt(jnp.mean(residual * residual, axis=-1, keepdims=True) + epsilon)
    return residual * inverse * norm_gain


def state_space(values, step_sizes, log_decay, inputs_b, outputs_c, skip_gain):
    seq_count, length = (values.shape[0], values.shape[1])
    blocks = length // BLOCK
    values_k = values.reshape(seq_count, blocks, BLOCK, HEADS, HEAD_DIM)
    steps_k = step_sizes.reshape(seq_count, blocks, BLOCK, HEADS)
    totals = jnp.cumsum(log_decay.reshape(seq_count, blocks, BLOCK, HEADS), axis=2)
    in_k = inputs_b.reshape(seq_count, blocks, BLOCK, STATE)
    out_k = outputs_c.reshape(seq_count, blocks, BLOCK, STATE)
    causal = (
        jnp.arange(BLOCK, dtype=jnp.int32)[:, None] >= jnp.arange(BLOCK, dtype=jnp.int32)[None, :]
    )[None, None, :, :, None]
    spread = totals[:, :, :, None, :] - totals[:, :, None, :, :]
    kernel = jnp.where(causal, jnp.exp(jnp.where(causal, spread, 0.0)), 0.0)
    inner_cb = jnp.einsum("skin,skjn->skij", out_k, in_k, precision=highest)
    weighted = inner_cb[..., None] * kernel * steps_k[:, :, None, :, :]
    local_part = jnp.einsum("skijh,skjhp->skihp", weighted, values_k, precision=highest)
    to_end = jnp.exp(totals[:, :, -1:, :] - totals) * steps_k
    scaled_values = values_k * to_end[..., None]
    block_states = jnp.einsum("skjhp,skjn->skhpn", scaled_values, in_k, precision=highest)
    carried = jnp.zeros((seq_count, HEADS, HEAD_DIM, STATE), jnp.float32)
    entering = []
    for block_index in range(blocks):
        entering.append(carried)
        carried = (
            jnp.exp(totals[:, block_index, -1, :])[:, :, None, None] * carried
            + block_states[:, block_index]
        )
    entering_all = jnp.stack(entering, axis=1)
    carried_part = (
        jnp.einsum("skin,skhpn->skihp", out_k, entering_all, precision=highest)
        * jnp.exp(totals)[..., None]
    )
    result = (local_part + carried_part).reshape(seq_count, length, HEADS, HEAD_DIM)
    return result + skip_gain[:, None] * values


def mixer_core(projected, dt_raw, conv_weight, conv_bias, dt_bias, decay_log, skip_gain, gate_gain):
    row_count = projected.shape[0]
    seq_count = row_count // BUCKET
    shaped = projected.reshape(seq_count, BUCKET, projected.shape[1])
    gate_part = shaped[:, :, :INNER]
    conv_input = shaped[:, :, INNER:]
    padded = jnp.pad(conv_input, ((0, 0), (CONV - 1, 0), (0, 0)))
    convolved = conv_bias + conv_weight[0] * padded[:, 0:BUCKET]
    for offset in range(1, CONV):
        convolved = convolved + conv_weight[offset] * padded[:, offset : offset + BUCKET]
    activated = jax.nn.silu(convolved)
    values = activated[:, :, :INNER].reshape(seq_count, BUCKET, HEADS, HEAD_DIM)
    inputs_b = activated[:, :, INNER : INNER + STATE]
    outputs_c = activated[:, :, INNER + STATE :]
    step_sizes = jax.nn.softplus(dt_raw.reshape(seq_count, BUCKET, HEADS) + dt_bias)
    log_decay = -jnp.exp(decay_log) * step_sizes
    scanned = state_space(values, step_sizes, log_decay, inputs_b, outputs_c, skip_gain).reshape(
        seq_count, BUCKET, INNER
    )
    gated_out = scanned * jax.nn.silu(gate_part)
    inverse = lax.rsqrt(jnp.mean(gated_out * gated_out, axis=-1, keepdims=True) + epsilon)
    return (gated_out * inverse * gate_gain).reshape(row_count, INNER)


def layer_forward(residual, params):
    norm_gain, in_weight, dt_weight, small_params, out_weight = params
    normed = front_norm(residual, norm_gain).astype(jnp.bfloat16)
    projected = jnp.dot(normed, in_weight, preferred_element_type=jnp.float32)
    dt_raw = jnp.dot(normed, dt_weight, preferred_element_type=jnp.float32)
    mixed_out = mixer_core(projected, dt_raw, *small_params).astype(jnp.bfloat16)
    output = residual + jnp.dot(mixed_out, out_weight, preferred_element_type=jnp.float32)
    return (output, (normed, projected, dt_raw, mixed_out))


def contract_rows(left, right):
    return lax.dot_general(
        left, right, (((0,), (0,)), ((), ())), preferred_element_type=jnp.float32
    )


def contract_cols(left, right):
    return lax.dot_general(
        left, right, (((1,), (1,)), ((), ())), preferred_element_type=jnp.float32
    )


def column_term(columns, grads):
    return contract_rows(columns, grads)


def reorder(columns, data_groups, owners):
    row_count, total_cols = columns.shape
    shaped = columns.reshape(row_count, owners, data_groups, total_cols // (owners * data_groups))
    return shaped.transpose(0, 2, 1, 3).reshape(row_count, total_cols)


def per_device(
    inputs,
    cotangent,
    lengths,
    norm_gain,
    in_weight,
    dt_weight,
    conv_weight,
    conv_bias,
    dt_bias,
    decay_log,
    skip_gain,
    gate_gain,
    out_weight,
):
    first_section = lax.axis_index("section") == 0
    full_in, full_dt, full_out = (
        lax.all_gather(in_weight[0], "fsdp", axis=0, tiled=True),
        lax.all_gather(dt_weight[0], "fsdp", axis=0, tiled=True),
        lax.all_gather(out_weight[0], "fsdp", axis=0, tiled=True),
    )
    small_params = (
        conv_weight[0],
        conv_bias[0],
        dt_bias[0],
        decay_log[0],
        skip_gain[0],
        gate_gain[0],
    )
    own_gain = norm_gain[0]
    params = (own_gain, full_in, full_dt, small_params, full_out)
    per_micro = inputs.shape[0] // MICRO
    row_count = per_micro * BUCKET
    model_width = inputs.shape[2]
    proj_cols = full_in.shape[1]
    data_groups = lax.axis_size("dp")
    owners = lax.axis_size("fsdp")
    positions = jnp.arange(BUCKET, dtype=jnp.int32)
    empty_rows = jnp.zeros((row_count, model_width), jnp.float32)

    def micro_rows(source, micro_index):
        return source[micro_index * per_micro : (micro_index + 1) * per_micro].reshape(
            row_count, model_width
        )

    def arrange(columns):
        return reorder(columns, data_groups, owners)

    layer_inputs = []
    results = []
    kept_all = []
    for section_tick in range(MICRO + 1):
        if section_tick > 0:
            arrived = passed_along(results[-1], "section", 1)
        else:
            arrived = empty_rows
        own_rows = micro_rows(inputs, section_tick) if section_tick < MICRO else empty_rows
        residual = jnp.where(first_section, own_rows, arrived)
        output, kept_values = layer_forward(residual, params)
        layer_inputs.append(residual)
        results.append(output)
        kept_all.append(kept_values)
    small_acc = (jnp.zeros(own_gain.shape, jnp.float32),) + tuple(
        (jnp.zeros(a.shape, jnp.float32) for a in small_params)
    )
    total_in = None
    total_out = None
    grads_back = []
    for section_tick in range(MICRO + 1):
        if section_tick > 0:
            returned = passed_along(grads_back[-1], "section", -1)
        else:
            returned = empty_rows
        if section_tick < MICRO:
            own_lengths = lengths[section_tick * per_micro : (section_tick + 1) * per_micro]
            live_rows = (positions[None, :] < own_lengths[:, None]).astype(jnp.float32)
            top_grad = micro_rows(cotangent, section_tick) * live_rows.reshape(row_count, 1)
        else:
            top_grad = empty_rows
        later_tick = min(section_tick + 1, MICRO)
        earlier = max(section_tick - 1, 0)
        grad_output = jnp.where(first_section, returned, top_grad)
        residual = jnp.where(first_section, layer_inputs[earlier], layer_inputs[later_tick])
        normed, projected, dt_raw, mixed_out = jax.tree.map(
            lambda a, b: jnp.where(first_section, a, b), kept_all[earlier], kept_all[later_tick]
        )
        grad_rounded = grad_output.astype(jnp.bfloat16)
        grad_mixed = contract_cols(grad_rounded, full_out)
        _, pull_mixer = jax.vjp(mixer_core, projected, dt_raw, *small_params)
        pulled = pull_mixer(grad_mixed)
        grad_proj = pulled[0].astype(jnp.bfloat16)
        grad_dt = pulled[1].astype(jnp.bfloat16)
        grad_cat = jnp.concatenate([grad_proj, grad_dt], axis=1)
        grad_normed = contract_cols(grad_proj, full_in) + contract_cols(grad_dt, full_dt)
        _, pull_front = jax.vjp(front_norm, residual, own_gain)
        grad_residual, grad_gain = pull_front(grad_normed)
        grads_back.append(grad_output + grad_residual)
        small_acc = tuple((a + b for a, b in zip(small_acc, (grad_gain,) + tuple(pulled[2:]))))
        normed_cols = arrange(normed)
        mixed_cols = arrange(mixed_out)
        part_in = lax.psum_scatter(
            column_term(normed_cols, grad_cat), ("dp", "fsdp"), scatter_dimension=0, tiled=True
        )
        part_out = lax.psum_scatter(
            column_term(mixed_cols, grad_rounded), ("dp", "fsdp"), scatter_dimension=0, tiled=True
        )
        total_in = part_in if total_in is None else total_in + part_in
        total_out = part_out if total_out is None else total_out + part_out
    owned_in, owned_out = (
        lax.all_gather(total_in, "dp", axis=0, tiled=True),
        lax.all_gather(total_out, "dp", axis=0, tiled=True),
    )
    small_total = lax.psum(small_acc, ("dp", "fsdp"))
    layer_out = jnp.concatenate(
        [
            jnp.where(first_section, results[m], results[m + 1]).reshape(
                per_micro, BUCKET, model_width
            )
            for m in range(MICRO)
        ],
        axis=0,
    )
    input_grad = jnp.concatenate(
        [
            jnp.where(first_section, grads_back[m + 1], grads_back[m]).reshape(
                per_micro, BUCKET, model_width
            )
            for m in range(MICRO)
        ],
        axis=0,
    )
    grad_in_part = owned_in[:, :proj_cols]
    grad_dt_part = owned_in[:, proj_cols:]
    return (
        layer_out[None],
        input_grad[None],
        small_total[0][None],
        grad_in_part[None],
        grad_dt_part[None],
        small_total[1][None],
        small_total[2][None],
        small_total[3][None],
        small_total[4][None],
        small_total[5][None],
        small_total[6][None],
        owned_out[None],
    )


def solution(mesh):
    in_specs = (
        P(("dp", "fsdp"), None, None),
        P(("dp", "fsdp"), None, None),
        P(("dp", "fsdp")),
        P("section", None),
        P("section", "fsdp", None),
        P("section", "fsdp", None),
        P("section", None, None),
        P("section", None),
        P("section", None),
        P("section", None),
        P("section", None),
        P("section", None),
        P("section", "fsdp", None),
    )
    out_specs = (
        P("section", ("dp", "fsdp"), None, None),
        P("section", ("dp", "fsdp"), None, None),
        P("section", None),
        P("section", "fsdp", None),
        P("section", "fsdp", None),
        P("section", None, None),
        P("section", None),
        P("section", None),
        P("section", None),
        P("section", None),
        P("section", None),
        P("section", "fsdp", None),
    )
    return jax.shard_map(
        per_device, mesh=mesh, in_specs=in_specs, out_specs=out_specs, check_vma=False
    )
```

profile of v0, /device:TPU:0, one launch (start us, length us, event | category | flops | bytes accessed | tf_op | source)
XLA Modules:
  0.0 1780.0 jit_solution(17367377292099813090)
XLA Ops:
  19.5 117.1 %all-gather.12.cloned.1.call-done = bf16[1,1536,6400]{2,1,0:T(8,128)(2,1)} async-done(((bf16[1,384,6400]{2,1,0:T(8,128)(2,1)}), bf16[1,1536,6400]{2,1,0:T(8,128)(2,1)}) %all-gather.12.cloned.1.call-update) | async-done | bytes 19660816 | tf_op jit(solution)/shard_map/all_gather | solution.py:138
  136.7 8.1 fusion.10
  184.4 18.1 %all-gather.14.cloned.1.call-done = bf16[1,3072,1536]{2,1,0:T(8,128)(2,1)} async-done(((bf16[1,768,1536]{2,1,0:T(8,128)(2,1)}), bf16[1,3072,1536]{2,1,0:T(8,128)(2,1)}) %all-gather.14.cloned.1.call-update) | async-done | bytes 9437200 | tf_op jit(solution)/shard_map/all_gather | solution.py:140
  214.1 14.1 collective-permute-done
  231.9 8.2 fusion.8
  310.2 8.7 fusion.396
  321.8 8.4 fusion.6
  370.8 7.8 bitcast_add_fusion.5
  388.8 9.2 fusion.241
  439.4 7.5 multiply_reduce_fusion.20
  464.4 10.0 fusion.225
  530.0 8.0 bitcast_add_fusion.3
  571.6 14.4 fusion.4
  611.8 7.9 fusion.240
  643.2 11.1 fusion.227
  681.2 8.2 fusion.344
  707.1 7.6 bitcast_add_fusion.1
  721.7 7.4 bitcast_add_fusion.2
  754.3 14.3 fusion.2
  784.1 8.0 fusion.404
  792.6 21.3 %add_add_fusion.1 = f32[3072,1536]{1,0:T(8,128)} fusion(f32[3072,1536]{1,0:T(8,128)} %fusion.396, f32[3072,1536]{1,0:T(8,128)} %fusion.404, bf16[128,3072]{0,1:T(8,128)(2,1)} %bitcast.975, f32[128,1536]{1,0:T(8,128)} %collective-permute-done.3, pred[]{:T(512)S(6)} %eq.9), kind=kOutput, calls=%fused_computation.13 | convolution fusion | flops 1217593344 | bytes 58195968 | tf_op jit(solution)/shard_map/dot_general | solution.py:100
  834.1 19.9 %fusion.213 = f32[1536,6448]{1,0:T(8,128)} fusion(bf16[128,1536]{0,1:T(8,128)(2,1)S(1)} %bitcast.1029, bf16[128,48]{1,0:T(8,128)(2,1)} %bitcast.1059, bf16[128,6400]{1,0:T(8,128)(2,1)} %copy-done.45), kind=kOutput, calls=%fused_computation.278 | convolution fusion | flops 2538758144 | bytes 41660416 | tf_op jit(solution)/shard_map/dot_general | solution.py:100
  854.0 17.7 fusion.217
  921.3 10.7 fusion.229
  948.3 7.7 fusion.359
  967.9 40.4 %add_add_fusion = f32[1536,6448]{1,0:T(8,128)} fusion(f32[1536,6448]{1,0:T(8,128)} %fusion.213, f32[1536,6448]{1,0:T(8,128)} %fusion.217, bf16[128,1536]{0,1:T(8,128)(2,1)S(1)} %bitcast.994, bf16[128,48]{1,0:T(8,128)(2,1)S(1)} %bitcast.1058, bf16[128,6400]{1,0:T(8,128)(2,1)S(1)} %fusion.232), kind=kOutput, calls=%fused_computation | convolution fusion | flops 2558566400 | bytes 120893440 | tf_op jit(solution)/shard_map/dot_general | solution.py:100
  1009.5 390.6 %reduce-scatter.3.cloned.1.call-done = f32[96,6448]{1,0:T(8,128)} async-done(((f32[1536,6448]{1,0:T(8,128)}), f32[96,6448]{1,0:T(8,128)}) %reduce-scatter.3.cloned.1.call-update) | async-done | bytes 2476048 | tf_op jit(solution)/shard_map/reduce_scatter | solution.py:221
  1414.6 10.4 fusion
  1433.2 56.9 %all-gather.10.cloned.1.call-done = f32[768,1536]{1,0:T(8,128)} async-done(((f32[192,1536]{1,0:T(8,128)}), f32[768,1536]{1,0:T(8,128)}) %all-gather.10.cloned.1.call-update) | async-done | bytes 4718608 | tf_op jit(solution)/shard_map/all_gather | solution.py:231
  1490.0 176.3 %all-gather.8.cloned.1.call-done = f32[384,6448]{1,0:T(8,128)} async-done(((f32[96,6448]{1,0:T(8,128)}), f32[384,6448]{1,0:T(8,128)}) %all-gather.8.cloned.1.call-update) | async-done | bytes 9904144 | tf_op jit(solution)/shard_map/all_gather | solution.py:230
  1666.3 8.3 slice_bitcast_fusion
  1676.3 83.1 %all-reduce.63.cloned.1.call-done = (f32[1,1536]{1,0:T(1,128)}, f32[1,4,3328]{2,1,0:T(4,128)}, f32[1,3328]{1,0:T(1,128)}, f32[1,48]{1,0:T(1,128)}, f32[1,48]{1,0...) async-done(((f32[1,1536]{1,0:T(1,128)}, f32[1,4,3328]{2,1,0:T(4,128)}, f32[1,3328]{1,0:T(1,128)}, f32[1,48]{1,0:T(1,128)}, f32[1,48]{1,0:T(1,128)}, ...) | async-done | bytes 85584 | tf_op jit(solution)/shard_map/psum | solution.py:233
  (941 shorter events, 614.5 us)
Async XLA Ops:
  7.2 129.5 %all-gather.12.cloned.1.call-start = ((), (), s32[]{:S(2)}) async-start(), calls=%async_computation.4 | async-start | bytes 24576000 | tf_op jit(solution)/shard_map/all_gather | solution.py:138
  8.0 194.5 %all-gather.14.cloned.1.call-start = ((), (), s32[]{:S(2)}) async-start(), calls=%async_computation.5 | async-start | bytes 11796480 | tf_op jit(solution)/shard_map/all_gather | solution.py:140
  8.7 1000.7 %reduce-scatter.5.cloned.1.call-start = ((), (), s32[]{:S(2)}) async-start(), calls=%async_computation.7 | async-start | bytes 20054016 | tf_op jit(solution)/shard_map/reduce_scatter | solution.py:224
  8.8 221.1 %copy-start.142 = (f32[1536]{0:T(1024)}, f32[1536]{0:T(1024)S(1)}, u32[]{:S(2)}) copy-start(f32[1536]{0:T(1024)S(1)} %reduce.80) | copy-start | bytes 18436
  8.9 137.6 %copy-start.211 = (f32[3328]{0:T(1024)}, f32[3328]{0:T(1024)S(1)}, u32[]{:S(2)}) copy-start(f32[3328]{0:T(1024)S(1)} %reduce.78) | copy-start | bytes 39940
  15.5 753.1 %copy-start.78 = (bf16[1,1536,48]{1,2,0:T(8,128)(2,1)}, bf16[1,1536,48]{1,2,0:T(8,128)(2,1)S(1)}, u32[]{:S(2)}) copy-start(bf16[1,1536,48]{1,2,0:T(8,128)(2,1)S(1)} %all-gather.1) | copy-start | bytes 442372
  15.7 129.1 %copy-start.261 = (f32[128]{0:T(128)}, f32[128]{0:T(128)S(1)}, u32[]{:S(2)}) copy-start(f32[128]{0:T(128)S(1)} %add_rsqrt_fusion.5) | copy-start | bytes 1540
  15.7 230.8 %copy-start.253 = (f32[48]{0:T(128)}, f32[48]{0:T(128)S(1)}, u32[]{:S(2)}) copy-start(f32[48]{0:T(128)S(1)} %bitcast_negate_fusion) | copy-start | bytes 580
  16.2 230.4 %copy-start.140 = (f32[128,48]{1,0:T(8,128)}, f32[128,48]{1,0:T(8,128)S(1)}, u32[]{:S(2)}) copy-start(f32[128,48]{1,0:T(8,128)S(1)} %get-tuple-element.253) | copy-start | bytes 73732
  19.3 268.4 %copy-start.135 = (f32[3072]{0:T(1024)}, f32[3072]{0:T(1024)S(1)}, u32[]{:S(2)}) copy-start(f32[3072]{0:T(1024)S(1)} %mul.1954) | copy-start | bytes 36868
  19.3 249.1 %copy-start.194 = (pred[64,64]{1,0:T(8,128)(4,1)}, pred[64,64]{1,0:T(8,128)(4,1)S(1)}, u32[]{:S(2)}) copy-start(pred[64,64]{1,0:T(8,128)(4,1)S(1)} %iota_compare_fusion) | copy-start | bytes 12292
  19.5 220.8 %copy-start.147 = (f32[3328]{0:T(1024)}, f32[3328]{0:T(1024)S(1)}, u32[]{:S(2)}) copy-start(f32[3328]{0:T(1024)S(1)} %get-tuple-element.111) | copy-start | bytes 39940
  19.5 220.8 %copy-start.152 = (f32[3328]{0:T(1024)}, f32[3328]{0:T(1024)S(1)}, u32[]{:S(2)}) copy-start(f32[3328]{0:T(1024)S(1)} %get-tuple-element.112) | copy-start | bytes 39940
  19.5 220.8 %copy-start.157 = (f32[3328]{0:T(1024)}, f32[3328]{0:T(1024)S(1)}, u32[]{:S(2)}) copy-start(f32[3328]{0:T(1024)S(1)} %get-tuple-element.113) | copy-start | bytes 39940
  19.5 220.8 %copy-start.162 = (f32[3328]{0:T(1024)}, f32[3328]{0:T(1024)S(1)}, u32[]{:S(2)}) copy-start(f32[3328]{0:T(1024)S(1)} %get-tuple-element.114) | copy-start | bytes 39940
  184.4 106.4 %copy-start.7 = (f32[1,128,3072]{2,1,0:T(8,128)}, f32[1,128,3072]{2,1,0:T(8,128)S(1)}, u32[]{:S(2)}) copy-start(f32[1,128,3072]{2,1,0:T(8,128)S(1)} %get-tuple-element.181) | copy-start | bytes 4718596
  184.4 23.2 %copy-start.257 = (f32[128]{0:T(128)}, f32[128]{0:T(128)S(1)}, u32[]{:S(2)}) copy-start(f32[128]{0:T(128)S(1)} %add_rsqrt_fusion.4) | copy-start | bytes 1540
  207.6 20.6 %collective-permute-start = (f32[128,1536]{1,0:T(8,128)S(1)}, f32[128,1536]{1,0:T(8,128)S(1)}, u32[]{:S(2)}, u32[]{:S(2)}) collective-permute-start(f32[128,1536]{1,0:T(8,128)S(1)} %fusion.150), channel_id=1, source_target_pairs={{0,16},{1,17},{2,18},{3,19},{4,20},{5,21},{6,22},{7,23},{8,24},{9,... | collective-permute-start | bytes 2359304 | tf_op jit(solution)/shard_map/ppermute | solution.py:21
  297.5 21.3 %collective-permute-start.1 = (f32[128,1536]{1,0:T(8,128)S(1)}, f32[128,1536]{1,0:T(8,128)S(1)}, u32[]{:S(2)}, u32[]{:S(2)}) collective-permute-start(f32[128,1536]{1,0:T(8,128)S(1)} %fusion.153), channel_id=1, source_target_pairs={{0,16},{1,17},{2,18},{3,19},{4,20},{5,21},{6,22},{7,23},{8,24},{9,... | collective-permute-start | bytes 2359304 | tf_op jit(solution)/shard_map/ppermute | solution.py:21
  321.8 28.3 %copy-start.98 = (bf16[128,1536]{1,0:T(8,128)(2,1)}, bf16[128,1536]{1,0:T(8,128)(2,1)S(1)}, u32[]{:S(2)}) copy-start(bf16[128,1536]{1,0:T(8,128)(2,1)S(1)} %get-tuple-element.127) | copy-start | bytes 1179652
  348.8 108.2 %copy-start.118 = (f32[1,128,128]{2,1,0:T(8,128)}, f32[1,128,128]{2,1,0:T(8,128)S(1)}, u32[]{:S(2)}) copy-start(f32[1,128,128]{2,1,0:T(8,128)S(1)} %get-tuple-element.213) | copy-start | bytes 196612
  354.2 109.9 %copy-start.2 = (f32[2,64,48,64]{3,2,1,0:T(8,128)}, f32[2,64,48,64]{3,2,1,0:T(8,128)S(1)}, u32[]{:S(2)}) copy-start(f32[2,64,48,64]{3,2,1,0:T(8,128)S(1)} %reshape.2331) | copy-start | bytes 4718596
  509.5 82.0 %copy-start.112 = (f32[1,128,128]{2,1,0:T(8,128)}, f32[1,128,128]{2,1,0:T(8,128)S(1)}, u32[]{:S(2)}) copy-start(f32[1,128,128]{2,1,0:T(8,128)S(1)} %get-tuple-element.201) | copy-start | bytes 196612
  589.5 20.9 %collective-permute-start.2 = (f32[128,1536]{1,0:T(8,128)}, f32[128,1536]{1,0:T(8,128)}, u32[]{:S(2)}, u32[]{:S(2)}) collective-permute-start(f32[128,1536]{1,0:T(8,128)} %fusion.374), channel_id=1, source_target_pairs={{16,0},{17,1},{18,2},{19,3},{20,4},{21,5},{22,6},{23,7},{24,8},{25... | collective-permute-start | bytes 2359304 | tf_op jit(solution)/shard_map/ppermute | solution.py:21
  772.7 19.9 %collective-permute-start.3 = (f32[128,1536]{1,0:T(8,128)}, f32[128,1536]{1,0:T(8,128)}, u32[]{:S(2)}, u32[]{:S(2)}) collective-permute-start(f32[128,1536]{1,0:T(8,128)} %get-tuple-element.146), channel_id=1, source_target_pairs={{16,0},{17,1},{18,2},{19,3},{20,4},{21,5},{22,6},{23,7},{24,8},{25... | collective-permute-start | bytes 2359304 | tf_op jit(solution)/shard_map/ppermute | solution.py:21
  813.9 586.2 %reduce-scatter.3.cloned.1.call-start = ((), (), s32[]{:S(2)}) async-start(), calls=%async_computation.6 | async-start | bytes 42614784 | tf_op jit(solution)/shard_map/reduce_scatter | solution.py:221
  834.1 37.6 %slice-start = ((s8[9437184]{0:T(1024)(128)(4,1)}), s8[4194304]{0:T(1024)(128)(4,1)S(1)}, s32[]{:S(2)}) async-start(s8[9437184]{0:T(1024)(128)(4,1)} %bitcast.961), calls=%async_computation.9 | async-start | bytes 8388608
  834.1 37.6 %slice-start.1 = ((s8[9437184]{0:T(1024)(128)(4,1)}), s8[4194304]{0:T(1024)(128)(4,1)S(1)}, s32[]{:S(2)}) async-start(s8[9437184]{0:T(1024)(128)(4,1)} %bitcast.961), calls=%async_computation.10 | async-start | bytes 8388608
  1008.4 481.6 %all-gather.10.cloned.1.call-start = ((), (), s32[]{:S(2)}) async-start(), calls=%async_computation.3 | async-start | bytes 5898240 | tf_op jit(solution)/shard_map/all_gather | solution.py:231
  1009.4 390.9 %copy-start.81 = (f32[128,1536]{1,0:T(8,128)S(1)}, f32[128,1536]{1,0:T(8,128)}, u32[]{:S(2)}) copy-start(f32[128,1536]{1,0:T(8,128)} %copy-done.80) | copy-start | bytes 2359300
  1009.5 656.8 %all-gather.8.cloned.1.call-start = ((), (), s32[]{:S(2)}) async-start(), calls=%async_computation.2 | async-start | bytes 12533760 | tf_op jit(solution)/shard_map/all_gather | solution.py:230
  1400.2 359.1 %all-reduce.63.cloned.1.call-start = ((), (), s32[]{:S(2)}) async-start(), calls=%async_computation.8 | async-start | bytes 173056 | tf_op jit(solution)/shard_map/psum | solution.py:233
  (276 other events, 1375.0 us)
Sparse Core Ops, SparseCore 0:
  9.6 127.0 all-gather.11
  138.2 64.2 all-gather.13
  814.1 195.3 reduce-scatter.4
  1013.6 386.4 reduce-scatter.2
  1401.6 88.4 all-gather.9
  1491.4 174.7 all-gather.7
  1671.8 87.5 all-reduce.62
where the time goes:
time: 1790 us; the launch traced here: 1780 us
  waiting for transfers between devices  865 us (48%)
  matrix products  454 us (25%)
  local copies, waits for them, and re-layouts  295 us (16%)
  other arithmetic  132 us (7%)
    reduce_scatter x1, waiting for transfers between devices, per_device(): lax.psum_scatter(column_term(normed_cols, grad_cat), ('dp', 'fsdp'), scat...  391 us
    all_gather x1, waiting for transfers between devices, per_device(): lax.all_gather(total_in, 'dp', axis=0, tiled=True)  176 us
    all_gather x1, waiting for transfers between devices, per_device(): lax.all_gather(in_weight[0], 'fsdp', axis=0, tiled=True)  117 us
    dot_general x6, matrix products, contract_rows(): lax.dot_general(left, right, (((0,), (0,)), ((), ())), preferred_element_...  116 us
    dot_general x12, matrix products, state_space(): jnp.einsum('skijh,skjhp->skihp', weighted, values_k, precision=highest)  93.3 us
    psum x1, waiting for transfers between devices, per_device(): small_total = lax.psum(small_acc, ('dp', 'fsdp'))  83.1 us
    dot_general x9, matrix products, contract_cols(): lax.dot_general(left, right, (((1,), (1,)), ((), ())), preferred_element_...  67 us
    dot_general x12, matrix products, state_space(): jnp.einsum('skjhp,skjn->skhpn', scaled_values, in_k, precision=highest)  65.5 us
  transfers between devices with their start and end apart: 11, of which 10 were waited for; matrix products, arithmetic and copies ran while one was open for 18% of the time, Pallas kernels for 0%

commit v1 on v0

--- a/solution.py
+++ b/solution.py
@@ -226,10 +226,16 @@
         )
         total_in = part_in if total_in is None else total_in + part_in
         total_out = part_out if total_out is None else total_out + part_out
-    owned_in, owned_out = (
-        lax.all_gather(total_in, "dp", axis=0, tiled=True),
-        lax.all_gather(total_out, "dp", axis=0, tiled=True),
-    )
+
+    def trees_see(vec):
+        group_axis = "dp"
+        k_all = lax.axis_size(group_axis)
+        nodes = tuple((k_all if ix == 0 else 1 for ix in range(vec.ndim)))
+        return lax.all_to_all(
+            jnp.tile(vec, nodes), group_axis, concat_axis=0, split_axis=0, tiled=True
+        )
+
+    owned_in, owned_out = (trees_see(total_in), lax.all_gather(total_out, "dp", axis=0, tiled=True))
     small_total = lax.psum(small_acc, ("dp", "fsdp"))
     layer_out = jnp.concatenate(
         [

time: 1790 us -> 1900 us (1.061)
  waiting for transfers between devices: 865 us -> 966 us
    reduce_scatter x1, waiting for transfers between devices: 0.98 us -> 338 us  [per_device(): lax.psum_scatter(column_term(mixed_cols, grad_rounded), ('dp', 'fsdp'), s...]
    all_gather x1 -> x0, waiting for transfers between devices: 176 us -> none  [per_device(): lax.all_gather(total_in, 'dp', axis=0, tiled=True)]
    reduce_scatter x1, waiting for transfers between devices: 391 us -> 322 us  [per_device(): lax.psum_scatter(column_term(normed_cols, grad_cat), ('dp', 'fsdp'), scat...]
    unnamed x603 -> x561, local copies, waits for them, and re-layouts: 48.6 us -> 45.7 us
  transfers between devices with their start and end apart: 11 -> 11, of which waited for: 10 -> 9; matrix products, arithmetic and copies ran while one was open for 18% -> 12% of each run, Pallas kernels for 0% -> 0%
where the time goes in v1:
time: 1900 us
  waiting for transfers between devices  966 us (51%)
  matrix products  463 us (24%)
  local copies, waits for them, and re-layouts  291 us (15%)
  other arithmetic  133 us (7%)
    reduce_scatter x1, waiting for transfers between devices, per_device(): lax.psum_scatter(column_term(mixed_cols, grad_rounded), ('dp', 'fsdp'), s...  338 us
    reduce_scatter x1, waiting for transfers between devices, per_device(): lax.psum_scatter(column_term(normed_cols, grad_cat), ('dp', 'fsdp'), scat...  322 us
    dot_general x6, matrix products, contract_rows(): lax.dot_general(left, right, (((0,), (0,)), ((), ())), preferred_element_...  125 us
    all_gather x1, waiting for transfers between devices, per_device(): lax.all_gather(in_weight[0], 'fsdp', axis=0, tiled=True)  118 us
    dot_general x12, matrix products, state_space(): jnp.einsum('skijh,skjhp->skihp', weighted, values_k, precision=highest)  92.9 us
    psum x1, waiting for transfers between devices, per_device(): small_total = lax.psum(small_acc, ('dp', 'fsdp'))  83.2 us
    dot_general x12, matrix products, state_space(): jnp.einsum('skjhp,skjn->skhpn', scaled_values, in_k, precision=highest)  67.5 us
    dot_general x9, matrix products, contract_cols(): lax.dot_general(left, right, (((1,), (1,)), ((), ())), preferred_element_...  67 us
  transfers between devices with their start and end apart: 11, of which 9 were waited for; matrix products, arithmetic and copies ran while one was open for 12% of the time, Pallas kernels for 0%

profile of v1, /device:TPU:0, one launch (start us, length us, event | category | flops | bytes accessed | tf_op | source)
XLA Modules:
  0.0 1895.3 jit_solution(7511097051946224348)
XLA Ops:
  18.9 117.8 %all-gather.9.cloned.1.call-done = bf16[1,1536,6400]{2,1,0:T(8,128)(2,1)} async-done(((bf16[1,384,6400]{2,1,0:T(8,128)(2,1)}), bf16[1,1536,6400]{2,1,0:T(8,128)(2,1)}) %all-gather.9.cloned.1.call-update) | async-done | bytes 19660816 | tf_op jit(solution)/shard_map/all_gather | solution.py:138
  136.7 8.1 fusion.10
  183.9 18.6 all-gather.11.cloned.1.call-done
  214.0 14.2 collective-permute-done
  231.8 8.2 fusion.8
  318.8 8.4 fusion.6
  367.7 8.0 bitcast_add_fusion.5
  385.8 9.2 fusion.241
  436.2 7.5 multiply_reduce_fusion.20
  461.2 10.0 fusion.225
  495.5 7.4 fusion.329
  526.3 7.9 bitcast_add_fusion.3
  567.8 13.8 fusion.4
  586.5 15.6 fusion.213
  631.1 7.9 fusion.240
  662.8 10.7 fusion.227
  699.8 8.2 fusion.344
  725.2 7.6 bitcast_add_fusion.1
  739.9 7.7 bitcast_add_fusion.2
  772.8 14.3 fusion.2
  792.4 17.8 fusion.217
  876.3 10.4 fusion.229
  912.9 40.1 %add_add_fusion = f32[1536,6448]{1,0:T(8,128)} fusion(f32[1536,6448]{1,0:T(8,128)} %fusion.213, f32[1536,6448]{1,0:T(8,128)} %fusion.217, bf16[128,1536]{0,1:T(8,128)(2,1)S(1)} %bitcast.995, bf16[128,48]{1,0:T(8,128)(2,1)S(1)} %bitcast.1059, bf16[128,6400]{1,0:T(8,128)(2,1)S(1)} %fusion.232), kind=kOutput, calls=%fused_computation | convolution fusion | flops 2558566400 | bytes 120893440 | tf_op jit(solution)/shard_map/dot_general | solution.py:100
  956.7 11.3 fusion.396
  978.9 11.8 fusion.404
  990.6 28.6 %add_add_fusion.1 = f32[3072,1536]{1,0:T(8,128)} fusion(f32[3072,1536]{1,0:T(8,128)} %fusion.396, f32[3072,1536]{1,0:T(8,128)} %fusion.404, bf16[128,3072]{0,1:T(8,128)(2,1)} %bitcast.976, f32[128,1536]{1,0:T(8,128)} %collective-permute-done.3, pred[]{:T(512)S(6)} %eq.9), kind=kOutput, calls=%fused_computation.13 | convolution fusion | flops 1217593344 | bytes 58195968 | tf_op jit(solution)/shard_map/dot_general | solution.py:100
  1019.3 321.8 %reduce-scatter.3.cloned.1.call-done = f32[96,6448]{1,0:T(8,128)} async-done(((f32[1536,6448]{1,0:T(8,128)}), f32[96,6448]{1,0:T(8,128)}) %reduce-scatter.3.cloned.1.call-update) | async-done | bytes 2476048 | tf_op jit(solution)/shard_map/reduce_scatter | solution.py:221
  1353.5 338.0 %reduce-scatter.5.cloned.1.call-done = f32[192,1536]{1,0:T(8,128)} async-done(((f32[3072,1536]{1,0:T(8,128)}), f32[192,1536]{1,0:T(8,128)}) %reduce-scatter.5.cloned.1.call-update) | async-done | bytes 1179664 | tf_op jit(solution)/shard_map/reduce_scatter | solution.py:224
  1701.4 10.9 fusion
  1720.4 61.0 %all-gather.7.cloned.1.call-done = f32[768,1536]{1,0:T(8,128)} async-done(((f32[192,1536]{1,0:T(8,128)}), f32[768,1536]{1,0:T(8,128)}) %all-gather.7.cloned.1.call-update) | async-done | bytes 4718608 | tf_op jit(solution)/shard_map/all_gather | solution.py:238
  1781.4 8.3 slice_bitcast_fusion
  1791.4 83.2 %all-reduce.63.cloned.1.call-done = (f32[1,1536]{1,0:T(1,128)}, f32[1,4,3328]{2,1,0:T(4,128)}, f32[1,3328]{1,0:T(1,128)}, f32[1,48]{1,0:T(1,128)}, f32[1,48]{1,0...) async-done(((f32[1,1536]{1,0:T(1,128)}, f32[1,4,3328]{2,1,0:T(4,128)}, f32[1,3328]{1,0:T(1,128)}, f32[1,48]{1,0:T(1,128)}, f32[1,48]{1,0:T(1,128)}, ...) | async-done | bytes 85584 | tf_op jit(solution)/shard_map/psum | solution.py:239
  (899 shorter events, 622.9 us)
Async XLA Ops:
  7.2 129.5 %all-gather.9.cloned.1.call-start = ((), (), s32[]{:S(2)}) async-start(), calls=%async_computation.4 | async-start | bytes 24576000 | tf_op jit(solution)/shard_map/all_gather | solution.py:138
  8.0 194.5 %all-gather.11.cloned.1.call-start = ((), (), s32[]{:S(2)}) async-start(), calls=%async_computation.5 | async-start | bytes 11796480 | tf_op jit(solution)/shard_map/all_gather | solution.py:140
  8.7 1332.4 %reduce-scatter.3.cloned.1.call-start = ((), (), s32[]{:S(2)}) async-start(), calls=%async_computation.6 | async-start | bytes 42614784 | tf_op jit(solution)/shard_map/reduce_scatter | solution.py:221
  8.8 221.0 %copy-start.135 = (f32[1536]{0:T(1024)}, f32[1536]{0:T(1024)S(1)}, u32[]{:S(2)}) copy-start(f32[1536]{0:T(1024)S(1)} %reduce.80) | copy-start | bytes 18436
  8.9 231.3 %copy-start.200 = (f32[3328]{0:T(1024)}, f32[3328]{0:T(1024)S(1)}, u32[]{:S(2)}) copy-start(f32[3328]{0:T(1024)S(1)} %reduce.78) | copy-start | bytes 39940
  15.5 771.6 %copy-start.78 = (bf16[1,1536,48]{1,2,0:T(8,128)(2,1)}, bf16[1,1536,48]{1,2,0:T(8,128)(2,1)S(1)}, u32[]{:S(2)}) copy-start(bf16[1,1536,48]{1,2,0:T(8,128)(2,1)S(1)} %all-gather.1) | copy-start | bytes 442372
  15.7 214.2 %copy-start.244 = (f32[128]{0:T(128)}, f32[128]{0:T(128)S(1)}, u32[]{:S(2)}) copy-start(f32[128]{0:T(128)S(1)} %add_rsqrt_fusion.5) | copy-start | bytes 1540
  15.7 284.7 %copy-start.237 = (f32[48]{0:T(128)}, f32[48]{0:T(128)S(1)}, u32[]{:S(2)}) copy-start(f32[48]{0:T(128)S(1)} %bitcast_negate_fusion) | copy-start | bytes 580
  18.6 266.6 %copy-start.127 = (f32[3072]{0:T(1024)}, f32[3072]{0:T(1024)S(1)}, u32[]{:S(2)}) copy-start(f32[3072]{0:T(1024)S(1)} %mul.1954) | copy-start | bytes 36868
  18.7 247.2 %copy-start.184 = (pred[64,64]{1,0:T(8,128)(4,1)}, pred[64,64]{1,0:T(8,128)(4,1)S(1)}, u32[]{:S(2)}) copy-start(pred[64,64]{1,0:T(8,128)(4,1)S(1)} %iota_compare_fusion) | copy-start | bytes 12292
  18.8 221.4 %copy-start.140 = (f32[3328]{0:T(1024)}, f32[3328]{0:T(1024)S(1)}, u32[]{:S(2)}) copy-start(f32[3328]{0:T(1024)S(1)} %get-tuple-element.99) | copy-start | bytes 39940
  18.8 221.4 %copy-start.145 = (f32[3328]{0:T(1024)}, f32[3328]{0:T(1024)S(1)}, u32[]{:S(2)}) copy-start(f32[3328]{0:T(1024)S(1)} %get-tuple-element.100) | copy-start | bytes 39940
  18.8 221.4 %copy-start.150 = (f32[3328]{0:T(1024)}, f32[3328]{0:T(1024)S(1)}, u32[]{:S(2)}) copy-start(f32[3328]{0:T(1024)S(1)} %get-tuple-element.101) | copy-start | bytes 39940
  18.8 221.4 %copy-start.155 = (f32[3328]{0:T(1024)}, f32[3328]{0:T(1024)S(1)}, u32[]{:S(2)}) copy-start(f32[3328]{0:T(1024)S(1)} %get-tuple-element.102) | copy-start | bytes 39940
  183.8 104.3 %copy-start.8 = (f32[1,128,3072]{2,1,0:T(8,128)}, f32[1,128,3072]{2,1,0:T(8,128)S(1)}, u32[]{:S(2)}) copy-start(f32[1,128,3072]{2,1,0:T(8,128)S(1)} %get-tuple-element.169) | copy-start | bytes 4718596
  183.9 104.3 %copy-start.241 = (f32[128]{0:T(128)}, f32[128]{0:T(128)S(1)}, u32[]{:S(2)}) copy-start(f32[128]{0:T(128)S(1)} %add_rsqrt_fusion.4) | copy-start | bytes 1540
  207.6 20.6 %collective-permute-start = (f32[128,1536]{1,0:T(8,128)S(1)}, f32[128,1536]{1,0:T(8,128)S(1)}, u32[]{:S(2)}, u32[]{:S(2)}) collective-permute-start(f32[128,1536]{1,0:T(8,128)S(1)} %fusion.150), channel_id=1, source_target_pairs={{0,16},{1,17},{2,18},{3,19},{4,20},{5,21},{6,22},{7,23},{8,24},{9,... | collective-permute-start | bytes 2359304 | tf_op jit(solution)/shard_map/ppermute | solution.py:21
  231.8 68.7 %copy-start.119 = (f32[128,48]{1,0:T(8,128)}, f32[128,48]{1,0:T(8,128)S(1)}, u32[]{:S(2)}) copy-start(f32[128,48]{1,0:T(8,128)S(1)} %get-tuple-element.242) | copy-start | bytes 73732
  295.0 20.9 %collective-permute-start.1 = (f32[128,1536]{1,0:T(8,128)S(1)}, f32[128,1536]{1,0:T(8,128)}, u32[]{:S(2)}, u32[]{:S(2)}) collective-permute-start(f32[128,1536]{1,0:T(8,128)S(1)} %fusion.153), channel_id=1, source_target_pairs={{0,16},{1,17},{2,18},{3,19},{4,20},{5,21},{6,22},{7,23},{8,24},{9,... | collective-permute-start | bytes 2359304 | tf_op jit(solution)/shard_map/ppermute | solution.py:21
  318.8 28.2 %copy-start.96 = (bf16[128,1536]{1,0:T(8,128)(2,1)}, bf16[128,1536]{1,0:T(8,128)(2,1)S(1)}, u32[]{:S(2)}) copy-start(bf16[128,1536]{1,0:T(8,128)(2,1)S(1)} %get-tuple-element.115) | copy-start | bytes 1179652
  345.7 108.1 %copy-start.110 = (f32[1,128,128]{2,1,0:T(8,128)}, f32[1,128,128]{2,1,0:T(8,128)S(1)}, u32[]{:S(2)}) copy-start(f32[1,128,128]{2,1,0:T(8,128)S(1)} %get-tuple-element.201) | copy-start | bytes 196612
  351.2 109.7 %copy-start.2 = (f32[2,64,48,64]{3,2,1,0:T(8,128)}, f32[2,64,48,64]{3,2,1,0:T(8,128)S(1)}, u32[]{:S(2)}) copy-start(f32[2,64,48,64]{3,2,1,0:T(8,128)S(1)} %reshape.2338) | copy-start | bytes 4718596
  505.8 122.0 %copy-start.106 = (f32[1,128,128]{2,1,0:T(8,128)}, f32[1,128,128]{2,1,0:T(8,128)S(1)}, u32[]{:S(2)}) copy-start(f32[1,128,128]{2,1,0:T(8,128)S(1)} %get-tuple-element.189) | copy-start | bytes 196612
  585.2 44.3 %collective-permute-start.2 = (f32[128,1536]{1,0:T(8,128)}, f32[128,1536]{1,0:T(8,128)}, u32[]{:S(2)}, u32[]{:S(2)}) collective-permute-start(f32[128,1536]{1,0:T(8,128)} %fusion.374), channel_id=1, source_target_pairs={{16,0},{17,1},{18,2},{19,3},{20,4},{21,5},{22,6},{23,7},{24,8},{25... | collective-permute-start | bytes 2359304 | tf_op jit(solution)/shard_map/ppermute | solution.py:21
  791.1 24.4 %collective-permute-start.3 = (f32[128,1536]{1,0:T(8,128)}, f32[128,1536]{1,0:T(8,128)}, u32[]{:S(2)}, u32[]{:S(2)}) collective-permute-start(f32[128,1536]{1,0:T(8,128)} %get-tuple-element.134), channel_id=1, source_target_pairs={{16,0},{17,1},{18,2},{19,3},{20,4},{21,5},{22,6},{23,7},{24,8},{25... | collective-permute-start | bytes 2359304 | tf_op jit(solution)/shard_map/ppermute | solution.py:21
  792.4 23.1 %slice-start = ((s8[9437184]{0:T(1024)(128)(4,1)}), s8[4194304]{0:T(1024)(128)(4,1)S(1)}, s32[]{:S(2)}) async-start(s8[9437184]{0:T(1024)(128)(4,1)} %bitcast.962), calls=%async_computation.9 | async-start | bytes 8388608
  792.4 23.1 %slice-start.1 = ((s8[9437184]{0:T(1024)(128)(4,1)}), s8[4194304]{0:T(1024)(128)(4,1)S(1)}, s32[]{:S(2)}) async-start(s8[9437184]{0:T(1024)(128)(4,1)} %bitcast.962), calls=%async_computation.10 | async-start | bytes 8388608
  953.0 738.4 %reduce-scatter.5.cloned.1.call-start = ((), (), s32[]{:S(2)}) async-start(), calls=%async_computation.7 | async-start | bytes 20054016 | tf_op jit(solution)/shard_map/reduce_scatter | solution.py:224
  1347.2 434.2 %all-to-all-start = ((f32[4,96,6448]{2,1,0:T(8,128)}), f32[4,96,6448]{2,1,0:T(8,128)}, u32[]{:S(2)}, u32[]{:S(2)}) async-start(f32[4,96,6448]{2,1,0:T(8,128)} %tile.2), calls=%async_computation | async-start | bytes 20054016 | tf_op jit(solution)/shard_map/all_to_all | solution.py:234
  1353.4 338.2 %copy-start.81 = (f32[128,1536]{1,0:T(8,128)S(1)}, f32[128,1536]{1,0:T(8,128)}, u32[]{:S(2)}) copy-start(f32[128,1536]{1,0:T(8,128)} %copy-done.80) | copy-start | bytes 2359300
  1353.4 428.0 %all-gather.7.cloned.1.call-start = ((), (), s32[]{:S(2)}) async-start(), calls=%async_computation.3 | async-start | bytes 5898240 | tf_op jit(solution)/shard_map/all_gather | solution.py:238
  1691.5 183.0 %all-reduce.63.cloned.1.call-start = ((), (), s32[]{:S(2)}) async-start(), calls=%async_computation.8 | async-start | bytes 173056 | tf_op jit(solution)/shard_map/psum | solution.py:239
  (255 other events, 1265.4 us)
Sparse Core Ops, SparseCore 0:
  9.6 127.0 all-gather.8
  138.2 64.2 all-gather.10
  953.1 387.9 reduce-scatter.2
  1345.1 346.3 reduce-scatter.4
  1692.9 88.4 all-gather.6
  1786.8 87.7 all-reduce.62
